TPU v7x, 32 devices: a whole 2x2x4 slice. The times are simulated.
32 devices in a mesh: feat: 4 (over y, x), ex: 8 (over z, core).
Axes of the slice: x: 2, y: 2, z: 4, core: 2. Of those that a mesh axis runs over, the one named last changes fastest.
Arguments:
- x_values: bfloat16 [8192, 8192], P('ex', 'feat'), may hold values from -6 to 9, as said below
- tile_live: int32 [64, 64], P('ex', 'feat'), may hold values from 0 to 1
- labels: int32 [8192], P('ex'), may hold values from 0 to 127
- margins: bfloat16 [8192, 128], P('ex'), may hold values from -6 to 240, as said below
- coef: float32 [2, 4096, 128], P(None, ('feat', 'ex')), may hold values from -1.2 to 1.2
- order: int32 [3, 4], P(None, 'feat'), may hold values from 0 to 1
Outputs:
- margins_out: float32 [8192, 128], P('ex')
- coef_out: float32 [2, 4096, 128], P(None, ('feat', 'ex'))
Inputs may be any that keep to these rules, and one draw needn't show every extreme that they name: `x_values`: feature values lie within this range. `margins`: start scores lie within this range.
All inputs are finite; a program needn't handle non-finite values.
Results may differ from a plain program's by a relative error of at most 0.0015.
Values may be sent and summed in bfloat16 or wider, within the bound.
No kernel may reach another device: no remote copies, remote signals or barrier semaphores. Data moves between devices by JAX's collectives and lax.ppermute only.
A program may use at most 64 MiB of HBM per device.

v0:
```python
import jax
import jax.numpy as jnp
from jax import lax
from jax.sharding import PartitionSpec as P

C = 128
BLOCK = 1024
STEPS = 3
ridge = 0.002
lasso = 0.005


def soft_parts(score, onehot):
    row_max = jnp.max(score, axis=1, keepdims=True)
    expo = jnp.exp(score - row_max)
    prob = expo / jnp.sum(expo, axis=1, keepdims=True)
    residual = (prob - onehot).astype(jnp.bfloat16)
    spread = (1.0 - jnp.sum(prob * prob, axis=1)).astype(jnp.bfloat16)
    return (residual, spread)


def proximal(old_rows, grad_sum, curv_sum, count):
    curv = curv_sum / count + ridge
    shifted = old_rows - grad_sum / count / curv[:, None]
    limit = (lasso / curv)[:, None]
    return shifted - jnp.clip(shifted, -limit, limit)


def local(x_values, tile_live, labels, margins, coef, order):
    rows_here = x_values.shape[0]
    count = rows_here * lax.axis_size("ex")
    rows_own = coef.shape[1]
    tiles = BLOCK // 128
    classes = jnp.arange(C, dtype=jnp.int32)
    onehot = (labels[:, None] == classes[None, :]).astype(jnp.float32)
    score = margins.astype(jnp.float32)
    for step in range(STEPS):
        residual, spread = soft_parts(score, onehot)
        chosen = order[step, 0]
        block_x = lax.dynamic_slice_in_dim(x_values, chosen * BLOCK, BLOCK, 1)
        live_tiles = lax.dynamic_slice_in_dim(tile_live, chosen * tiles, tiles, 1).astype(
            jnp.bfloat16
        )
        block_x = (
            block_x.reshape(rows_here // 128, 128, tiles, 128) * live_tiles[:, None, :, None]
        ).reshape(rows_here, BLOCK)
        squares = block_x * block_x
        grad_part = lax.dot_general(
            block_x, residual, (((0,), (0,)), ((), ())), preferred_element_type=jnp.float32
        )
        curv_part = jnp.dot(spread, squares, preferred_element_type=jnp.float32)
        old_rows = lax.dynamic_index_in_dim(coef, chosen, 0, keepdims=False)
        grad_sum, curv_sum = lax.psum((grad_part, curv_part), "ex")
        old_block = lax.all_gather(old_rows, "ex", axis=0, tiled=True)
        new_block = proximal(old_block, grad_sum, curv_sum, count)
        step_delta = (new_block - old_block).astype(jnp.bfloat16)
        own_start = lax.axis_index("ex") * rows_own
        new_rows = lax.dynamic_slice_in_dim(new_block, own_start, rows_own, 0)
        coef = lax.dynamic_update_index_in_dim(coef, new_rows, chosen, 0)
        contrib = jnp.dot(block_x, step_delta, preferred_element_type=jnp.float32)
        score = score + lax.psum(contrib, "feat")
    return (score, coef)


def solution(mesh):
    return jax.shard_map(
        local,
        mesh=mesh,
        in_specs=(
            P("ex", "feat"),
            P("ex", "feat"),
            P("ex"),
            P("ex", None),
            P(None, ("feat", "ex"), None),
            P(None, "feat"),
        ),
        out_specs=(P("ex", None), P(None, ("feat", "ex"), None)),
        check_vma=False,
    )
```

profile of v0, /device:TPU:0, one launch (start us, length us, event | category | flops | bytes accessed | tf_op | source)
XLA Modules:
  0.0 367.0 jit_solution(16654294411127184689)
XLA Ops:
  19.0 4.4 %bitcast_multiply_fusion = (bf16[1024,1024]{1,0:T(8,128)(2,1)S(1)}, bf16[1024,1024]{1,0:T(8,128)(2,1)S(1)}, bf16[1024,1024]{1,0:T(8,128)(2,1)}) fusion(bf16[128,8,8,128]{3,2,1,0:T(8,128)(2,1)S(1)} %bitcast.59, bf16[1024,2048]{1,0:T(8,128)(2,1)S(1)} %copy-done.3, s32[]{:T(128)S(6)} %select_n.44, bf16[128,8,8,128]{3,2,1,0:T(8,128)(2,1)S(1)} %bitcast.57, ...), kind=kLoop, calls=%fused_computation | loop fusion | flops 12582912 | bytes 18874380 | tf_op jit(solution)/shard_map/mul | solution.py:45
  24.7 2.1 fusion.19
  28.0 2.0 fusion.4
  30.0 18.2 %psum.64 = f32[1024]{0:T(1024)S(1)} all-reduce(f32[1024]{0:T(1024)S(1)} %bitcast.60), channel_id=1, replica_groups=mesh['feat'=4,'ex'=8] {'ex'}, use_global_device_ids=true, to_apply=%region_4.5 | all-reduce | flops 1024 | bytes 8192 | tf_op jit(solution)/shard_map/psum | solution.py:53
  49.5 14.9 %all-gather = f32[1,1024,128]{2,1,0:T(8,128)S(1)} all-gather(f32[1,128,128]{2,1,0:T(8,128)S(1)} %constant_dynamic-slice_fusion.2), channel_id=2, replica_groups=mesh['feat'=4,'ex'=8] {'ex'}, dimensions={1}, use_global_device_ids=true | all-gather | bytes 589824 | tf_op jit(solution)/shard_map/all_gather | solution.py:54
  64.4 21.9 %all-reduce.7.cloned.1.call-done = f32[1024,128]{1,0:T(8,128)} async-done(((f32[1024,128]{1,0:T(8,128)}), f32[1024,128]{1,0:T(8,128)}) %all-reduce.7.cloned.1.call-update) | async-done | bytes 524304 | tf_op jit(solution)/shard_map/psum | solution.py:53
  87.9 3.1 fusion.21
  92.7 14.8 %all-gather.1 = f32[1,1024,128]{2,1,0:T(8,128)S(1)} all-gather(f32[1,128,128]{2,1,0:T(8,128)S(1)} %constant_dynamic-slice_fusion), channel_id=3, replica_groups=mesh['feat'=4,'ex'=8] {'ex'}, dimensions={1}, use_global_device_ids=true | all-gather | bytes 589824 | tf_op jit(solution)/shard_map/all_gather | solution.py:54
  107.6 27.9 %all-reduce.9.cloned.1.call-done = f32[1024,128]{1,0:T(8,128)} async-done(((f32[1024,128]{1,0:T(8,128)}), f32[1024,128]{1,0:T(8,128)}) %all-reduce.9.cloned.1.call-update) | async-done | bytes 524304 | tf_op jit(solution)/shard_map/psum | solution.py:61
  138.3 1.5 multiply_reduce_fusion.1
  139.9 3.1 fusion.29
  143.0 2.0 fusion.2
  145.0 16.3 %psum.67 = f32[1024]{0:T(1024)S(1)} all-reduce(f32[1024]{0:T(1024)S(1)} %bitcast.61), channel_id=1, replica_groups=mesh['feat'=4,'ex'=8] {'ex'}, use_global_device_ids=true, to_apply=%region_10.11 | all-reduce | flops 1024 | bytes 8192 | tf_op jit(solution)/shard_map/psum | solution.py:53
  161.3 38.0 %all-reduce.11.cloned.1.call-done = f32[1024,128]{1,0:T(8,128)} async-done(((f32[1024,128]{1,0:T(8,128)}), f32[1024,128]{1,0:T(8,128)}) %all-reduce.11.cloned.1.call-update) | async-done | bytes 524304 | tf_op jit(solution)/shard_map/psum | solution.py:53
  199.3 1.5 minimum_subtract_fusion.1
  201.6 3.2 fusion.23
  207.7 15.9 %all-gather.2 = f32[1,1024,128]{2,1,0:T(8,128)} all-gather(f32[1,128,128]{2,1,0:T(8,128)S(1)} %constant_dynamic-slice_fusion.1), channel_id=4, replica_groups=mesh['feat'=4,'ex'=8] {'ex'}, dimensions={1}, use_global_device_ids=true | all-gather | bytes 589824 | tf_op jit(solution)/shard_map/all_gather | solution.py:54
  223.6 25.7 %all-reduce.13.cloned.1.call-done = f32[1024,128]{1,0:T(8,128)} async-done(((f32[1024,128]{1,0:T(8,128)}), f32[1024,128]{1,0:T(8,128)}) %all-reduce.13.cloned.1.call-update) | async-done | bytes 524304 | tf_op jit(solution)/shard_map/psum | solution.py:61
  251.4 2.1 fusion.27
  254.0 16.2 %psum.70 = f32[1024]{0:T(1024)S(1)} all-reduce(f32[1024]{0:T(1024)S(1)} %bitcast.62), channel_id=1, replica_groups=mesh['feat'=4,'ex'=8] {'ex'}, use_global_device_ids=true, to_apply=%region_16.17 | all-reduce | flops 1024 | bytes 8192 | tf_op jit(solution)/shard_map/psum | solution.py:53
  270.1 39.7 %all-reduce.15.cloned.1.call-done = f32[1024,128]{1,0:T(8,128)} async-done(((f32[1024,128]{1,0:T(8,128)}), f32[1024,128]{1,0:T(8,128)}) %all-reduce.15.cloned.1.call-update) | async-done | bytes 524304 | tf_op jit(solution)/shard_map/psum | solution.py:53
  309.9 1.5 minimum_subtract_fusion
  314.6 43.6 %all-reduce.17.cloned.1.call-done = f32[1024,128]{1,0:T(8,128)} async-done(((f32[1024,128]{1,0:T(8,128)}), f32[1024,128]{1,0:T(8,128)}) %all-reduce.17.cloned.1.call-update) | async-done | bytes 524304 | tf_op jit(solution)/shard_map/psum | solution.py:61
  358.2 1.9 add.88
  (65 shorter events, 22.0 us)
Async XLA Ops:
  7.2 79.2 %all-reduce.7.cloned.1.call-start = ((), (), s32[]{:S(2)}) async-start(), calls=%async_computation | async-start | bytes 1048576 | tf_op jit(solution)/shard_map/psum | solution.py:53
  16.8 2.2 copy-start.3
  19.0 5.7 %copy-start.2 = (bf16[1024,128]{1,0:T(8,128)(2,1)S(1)}, bf16[1024,128]{1,0:T(8,128)(2,1)}, u32[]{:S(2)}) copy-start(bf16[1024,128]{1,0:T(8,128)(2,1)} %param.9) | copy-start | bytes 786436
  19.0 5.7 %copy-start.9 = (s32[1024]{0:T(1024)S(1)}, s32[1024]{0:T(1024)}, u32[]{:S(2)}) copy-start(s32[1024]{0:T(1024)} %param.8) | copy-start | bytes 12292
  23.4 1.3 copy-start.1
  26.8 108.6 %all-reduce.9.cloned.1.call-start = ((), (), s32[]{:S(2)}) async-start(), calls=%async_computation.1 | async-start | bytes 1048576 | tf_op jit(solution)/shard_map/psum | solution.py:61
  91.0 108.3 %all-reduce.11.cloned.1.call-start = ((), (), s32[]{:S(2)}) async-start(), calls=%async_computation.2 | async-start | bytes 1048576 | tf_op jit(solution)/shard_map/psum | solution.py:53
  135.5 4.4 %copy-start = (bf16[1024,1024]{1,0:T(8,128)(2,1)S(1)}, bf16[1024,1024]{1,0:T(8,128)(2,1)}, u32[]{:S(2)}) copy-start(bf16[1024,1024]{1,0:T(8,128)(2,1)} %get-tuple-element.6) | copy-start | bytes 6291460
  143.0 106.3 %all-reduce.13.cloned.1.call-start = ((), (), s32[]{:S(2)}) async-start(), calls=%async_computation.3 | async-start | bytes 1048576 | tf_op jit(solution)/shard_map/psum | solution.py:61
  200.8 0.8 copy-start.6
  201.6 47.6 %copy-start.4 = (f32[1024,128]{1,0:T(8,128)S(1)}, f32[1024,128]{1,0:T(8,128)}, u32[]{:S(2)}) copy-start(f32[1024,128]{1,0:T(8,128)} %all-reduce.9.cloned.1.call-done) | copy-start | bytes 1572868
  204.8 105.1 %all-reduce.15.cloned.1.call-start = ((), (), s32[]{:S(2)}) async-start(), calls=%async_computation.4 | async-start | bytes 1048576 | tf_op jit(solution)/shard_map/psum | solution.py:53
  253.5 56.4 %copy-start.5 = (f32[1,1024,128]{2,1,0:T(8,128)S(1)}, f32[1,1024,128]{2,1,0:T(8,128)}, u32[]{:S(2)}) copy-start(f32[1,1024,128]{2,1,0:T(8,128)} %all-gather.2) | copy-start | bytes 1572868
  253.5 104.7 %all-reduce.17.cloned.1.call-start = ((), (), s32[]{:S(2)}) async-start(), calls=%async_computation.5 | async-start | bytes 1048576 | tf_op jit(solution)/shard_map/psum | solution.py:61
  311.4 0.8 copy-start.7
  314.6 45.5 %copy-start.8 = (f32[2,128,128]{2,1,0:T(8,128)}, f32[2,128,128]{2,1,0:T(8,128)S(1)}, u32[]{:S(2)}) copy-start(f32[2,128,128]{2,1,0:T(8,128)S(1)} %bitcast_dynamic-update-slice_fusion) | copy-start | bytes 393220
Sparse Core Ops, SparseCore 0:
  26.9 59.3 all-reduce.6
  91.1 44.3 all-reduce.8
  143.1 56.1 all-reduce.10
  204.9 44.2 all-reduce.12
  253.7 56.1 all-reduce.14
  313.9 44.3 all-reduce.16
where the time goes:
time: 368 us; the launch traced here: 367 us
  waiting for transfers between devices  197 us (54%)
  blocking collectives  96.2 us (26%)
  between operations  23.5 us (6%)
  other arithmetic  21.1 us (6%)
  matrix products  19.3 us (5%)
  local copies, waits for them, and re-layouts  9.45 us (3%)
    psum x3, waiting for transfers between devices, local(): grad_sum, curv_sum = lax.psum((grad_part, curv_part), 'ex')  99.7 us
    psum x3, waiting for transfers between devices, local(): score = score + lax.psum(contrib, 'feat')  97.2 us
    psum x3, blocking collectives, local(): grad_sum, curv_sum = lax.psum((grad_part, curv_part), 'ex')  50.6 us
    all_gather x3, blocking collectives, local(): old_block = lax.all_gather(old_rows, 'ex', axis=0, tiled=True)  45.7 us
    dot_general x3, matrix products, local(): contrib = jnp.dot(block_x, step_delta, preferred_element_type=jnp.float32)  7.76 us
  transfers between devices with their start and end apart: 6, of which 6 were waited for; matrix products, arithmetic and copies ran while one was open for 2% of the time, Pallas kernels for 0%

commit v1 on v0

--- a/solution.py
+++ b/solution.py
@@ -51,7 +51,8 @@
         curv_part = jnp.dot(spread, squares, preferred_element_type=jnp.float32)
         old_rows = lax.dynamic_index_in_dim(coef, chosen, 0, keepdims=False)
         grad_sum, curv_sum = lax.psum((grad_part, curv_part), "ex")
-        old_block = lax.all_gather(old_rows, "ex", axis=0, tiled=True)
+        copies = jnp.concatenate([old_rows] * lax.axis_size("ex"), axis=0)
+        old_block = lax.all_to_all(copies, "ex", 0, 0, tiled=True)
         new_block = proximal(old_block, grad_sum, curv_sum, count)
         step_delta = (new_block - old_block).astype(jnp.bfloat16)
         own_start = lax.axis_index("ex") * rows_own

time: 368 us -> 376 us (1.022)
  blocking collectives: 96.2 us -> 49.7 us
  waiting for transfers between devices: 197 us -> 226 us
  starting transfers between devices: 0.25 us -> 14.4 us
  local copies, waits for them, and re-layouts: 9.45 us -> 22.3 us
    all_gather x3 -> x0, blocking collectives: 45.7 us -> none  [local(): old_block = lax.all_gather(old_rows, 'ex', axis=0, tiled=True)]
    psum x3, waiting for transfers between devices: 97.2 us -> 115 us  [local(): score = score + lax.psum(contrib, 'feat')]
    all_to_all x0 -> x3, starting transfers between devices: none -> 14 us  [local(): old_block = lax.all_to_all(copies, 'ex', 0, 0, tiled=True)]
    unnamed x21 -> x38, local copies, waits for them, and re-layouts: 5.32 us -> 17.1 us
    psum x3, waiting for transfers between devices: 99.7 us -> 111 us  [local(): grad_sum, curv_sum = lax.psum((grad_part, curv_part), 'ex')]
    convert_element_type x0 -> x3, other arithmetic: none -> 5.59 us  [local(): step_delta = (new_block - old_block).astype(jnp.bfloat16)]
    sub x3 -> x0, other arithmetic: 4.53 us -> none  [proximal(): return shifted - jnp.clip(shifted, -limit, limit)]
  transfers between devices with their start and end apart: 6 -> 9, of which waited for: 6 -> 6; matrix products, arithmetic and copies ran while one was open for 2% -> 9% of each run, Pallas kernels for 0% -> 0%
where the time goes in v1:
time: 376 us; the launch traced here: 375 us
  waiting for transfers between devices  226 us (60%)
  blocking collectives  49.7 us (13%)
  between operations  24.3 us (6%)
  local copies, waits for them, and re-layouts  22.3 us (6%)
  matrix products  20 us (5%)
  other arithmetic  18.3 us (5%)
  starting transfers between devices  14.4 us (4%)
    psum x3, waiting for transfers between devices, local(): score = score + lax.psum(contrib, 'feat')  115 us
    psum x3, waiting for transfers between devices, local(): grad_sum, curv_sum = lax.psum((grad_part, curv_part), 'ex')  111 us
    psum x3, blocking collectives, local(): grad_sum, curv_sum = lax.psum((grad_part, curv_part), 'ex')  49.7 us
    unnamed x38, local copies, waits for them, and re-layouts  17.1 us
    all_to_all x3, starting transfers between devices, local(): old_block = lax.all_to_all(copies, 'ex', 0, 0, tiled=True)  14 us
    dot_general x3, matrix products, local(): lax.dot_general(block_x, residual, (((0,), (0,)), ((), ())), preferred_el...  7.95 us
    dot_general x3, matrix products, local(): contrib = jnp.dot(block_x, step_delta, preferred_element_type=jnp.float32)  7.7 us
  transfers between devices with their start and end apart: 9, of which 6 were waited for; matrix products, arithmetic and copies ran while one was open for 9% of the time, Pallas kernels for 0%

profile of v1, /device:TPU:0, one launch (start us, length us, event | category | flops | bytes accessed | tf_op | source)
XLA Modules:
  0.0 374.5 jit_solution(10226785791693824461)
XLA Ops:
  16.7 6.3 %all-to-all-start = ((f32[8,128,128]{2,1,0:T(8,128)}), f32[8,128,128]{2,1,0:T(8,128)S(1)}, u32[]{:S(2)}, u32[]{:S(2)}) async-start(f32[8,128,128]{2,1,0:T(8,128)} %bitcast.2), calls=%async_computation | async-start | bytes 1048576 | tf_op jit(solution)/shard_map/all_to_all | solution.py:55
  30.2 4.4 %bitcast_multiply_fusion = (bf16[1024,1024]{1,0:T(8,128)(2,1)S(1)}, bf16[1024,1024]{1,0:T(8,128)(2,1)S(1)}, bf16[1024,1024]{1,0:T(8,128)(2,1)}) fusion(bf16[128,8,8,128]{3,2,1,0:T(8,128)(2,1)S(1)} %bitcast.92, bf16[1024,2048]{1,0:T(8,128)(2,1)S(1)} %copy-done.3, s32[]{:T(128)S(6)} %select_n.44, bf16[128,8,8,128]{3,2,1,0:T(8,128)(2,1)S(1)} %bitcast.90, ...), kind=kLoop, calls=%fused_computation | loop fusion | flops 12582912 | bytes 18874380 | tf_op jit(solution)/shard_map/mul | solution.py:45
  35.9 2.1 fusion.19
  38.6 2.0 fusion.4
  44.4 17.1 %psum.64 = f32[1024]{0:T(1024)S(1)} all-reduce(f32[1024]{0:T(1024)S(1)} %bitcast.93), channel_id=1, replica_groups=mesh['feat'=4,'ex'=8] {'ex'}, use_global_device_ids=true, to_apply=%region_4.5 | all-reduce | flops 1024 | bytes 8192 | tf_op jit(solution)/shard_map/psum | solution.py:53
  61.6 34.2 %all-reduce.7.cloned.1.call-done = f32[1024,128]{1,0:T(8,128)} async-done(((f32[1024,128]{1,0:T(8,128)}), f32[1024,128]{1,0:T(8,128)}) %all-reduce.7.cloned.1.call-update) | async-done | bytes 524304 | tf_op jit(solution)/shard_map/psum | solution.py:53
  95.7 1.6 fusion.14
  97.3 3.1 fusion.40
  105.5 3.5 all-to-all-start.1
  109.1 35.8 %all-reduce.9.cloned.1.call-done = f32[1024,128]{1,0:T(8,128)} async-done(((f32[1024,128]{1,0:T(8,128)}), f32[1024,128]{1,0:T(8,128)}) %all-reduce.9.cloned.1.call-update) | async-done | bytes 524304 | tf_op jit(solution)/shard_map/psum | solution.py:62
  147.6 3.8 %fusion.23 = f32[1024,128]{1,0:T(8,128)} fusion(bf16[1024,1024]{1,0:T(8,128)(2,1)} %get-tuple-element.12, s32[1024]{0:T(1024)S(1)} %copy-done.6, f32[1024]{0:T(1024)S(1)} %fusion.16, f32[1024]{0:T(1024)S(1)} %fusion.31, f32[1024,128]{1,0:T(8,128)} %all-reduce.9.cloned.1.call-done, bf16[1024,128]{1,0:T(8,128)(2,1)S(1)} %copy-done.2), kind=kOutput, calls=%fused_computation.44 | convolution fusion | flops 269484032 | bytes 3420160 | tf_op jit(solution)/shard_map/dot_general | solution.py:48
  151.9 2.0 fusion.2
  153.9 16.3 %psum.67 = f32[1024]{0:T(1024)S(1)} all-reduce(f32[1024]{0:T(1024)S(1)} %bitcast.94), channel_id=1, replica_groups=mesh['feat'=4,'ex'=8] {'ex'}, use_global_device_ids=true, to_apply=%region_10.11 | all-reduce | flops 1024 | bytes 8192 | tf_op jit(solution)/shard_map/psum | solution.py:53
  170.2 37.5 %all-reduce.11.cloned.1.call-done = f32[1024,128]{1,0:T(8,128)} async-done(((f32[1024,128]{1,0:T(8,128)}), f32[1024,128]{1,0:T(8,128)}) %all-reduce.11.cloned.1.call-update) | async-done | bytes 524304 | tf_op jit(solution)/shard_map/psum | solution.py:53
  207.7 2.4 fusion.13
  210.1 3.1 fusion.41
  219.1 4.1 %all-to-all-start.2 = ((f32[8,128,128]{2,1,0:T(8,128)}), f32[8,128,128]{2,1,0:T(8,128)}, u32[]{:S(2)}, u32[]{:S(2)}) async-start(f32[8,128,128]{2,1,0:T(8,128)} %bitcast.14), calls=%async_computation.2 | async-start | bytes 1048576 | tf_op jit(solution)/shard_map/all_to_all | solution.py:55
  223.5 34.2 %all-reduce.13.cloned.1.call-done = f32[1024,128]{1,0:T(8,128)} async-done(((f32[1024,128]{1,0:T(8,128)}), f32[1024,128]{1,0:T(8,128)}) %all-reduce.13.cloned.1.call-update) | async-done | bytes 524304 | tf_op jit(solution)/shard_map/psum | solution.py:62
  259.3 2.1 fusion.21
  262.4 16.3 %psum.70 = f32[1024]{0:T(1024)S(1)} all-reduce(f32[1024]{0:T(1024)S(1)} %bitcast.95), channel_id=1, replica_groups=mesh['feat'=4,'ex'=8] {'ex'}, use_global_device_ids=true, to_apply=%region_16.17 | all-reduce | flops 1024 | bytes 8192 | tf_op jit(solution)/shard_map/psum | solution.py:53
  278.7 39.0 %all-reduce.15.cloned.1.call-done = f32[1024,128]{1,0:T(8,128)} async-done(((f32[1024,128]{1,0:T(8,128)}), f32[1024,128]{1,0:T(8,128)}) %all-reduce.15.cloned.1.call-update) | async-done | bytes 524304 | tf_op jit(solution)/shard_map/psum | solution.py:53
  317.7 1.7 fusion.12
  321.0 44.8 %all-reduce.17.cloned.1.call-done = f32[1024,128]{1,0:T(8,128)} async-done(((f32[1024,128]{1,0:T(8,128)}), f32[1024,128]{1,0:T(8,128)}) %all-reduce.17.cloned.1.call-update) | async-done | bytes 524304 | tf_op jit(solution)/shard_map/psum | solution.py:62
  365.8 1.9 add.88
  (85 shorter events, 31.1 us)
Async XLA Ops:
  7.2 20.4 %copy-start.5 = (s32[8,16]{1,0:T(8,128)S(1)}, s32[8,16]{1,0:T(8,128)}, u32[]{:S(2)}) copy-start(s32[8,16]{1,0:T(8,128)} %param.7) | copy-start | bytes 1540
  7.2 19.8 %copy-start.2 = (bf16[1024,128]{1,0:T(8,128)(2,1)S(1)}, bf16[1024,128]{1,0:T(8,128)(2,1)}, u32[]{:S(2)}) copy-start(bf16[1024,128]{1,0:T(8,128)(2,1)} %param.9) | copy-start | bytes 786436
  16.7 79.1 %all-to-all-start = ((f32[8,128,128]{2,1,0:T(8,128)}), f32[8,128,128]{2,1,0:T(8,128)S(1)}, u32[]{:S(2)}, u32[]{:S(2)}) async-start(f32[8,128,128]{2,1,0:T(8,128)} %bitcast.2), calls=%async_computation | async-start | bytes 1048576 | tf_op jit(solution)/shard_map/all_to_all | solution.py:55
  23.0 72.7 %all-reduce.7.cloned.1.call-start = ((), (), s32[]{:S(2)}) async-start(), calls=%async_computation.3 | async-start | bytes 1048576 | tf_op jit(solution)/shard_map/psum | solution.py:53
  28.0 2.2 copy-start.3
  30.2 5.7 %copy-start.6 = (s32[1024]{0:T(1024)S(1)}, s32[1024]{0:T(1024)}, u32[]{:S(2)}) copy-start(s32[1024]{0:T(1024)} %param.8) | copy-start | bytes 12292
  34.6 1.3 copy-start.1
  38.0 106.9 %all-reduce.9.cloned.1.call-start = ((), (), s32[]{:S(2)}) async-start(), calls=%async_computation.4 | async-start | bytes 1048576 | tf_op jit(solution)/shard_map/psum | solution.py:62
  105.5 102.2 %all-to-all-start.1 = ((f32[8,128,128]{2,1,0:T(8,128)}), f32[8,128,128]{2,1,0:T(8,128)S(1)}, u32[]{:S(2)}, u32[]{:S(2)}) async-start(f32[8,128,128]{2,1,0:T(8,128)} %bitcast.8), calls=%async_computation.1 | async-start | bytes 1048576 | tf_op jit(solution)/shard_map/all_to_all | solution.py:55
  109.0 98.7 %all-reduce.11.cloned.1.call-start = ((), (), s32[]{:S(2)}) async-start(), calls=%async_computation.5 | async-start | bytes 1048576 | tf_op jit(solution)/shard_map/psum | solution.py:53
  147.5 3.9 %copy-start.4 = (f32[1024,128]{1,0:T(8,128)S(1)}, f32[1024,128]{1,0:T(8,128)}, u32[]{:S(2)}) copy-start(f32[1024,128]{1,0:T(8,128)} %all-reduce.9.cloned.1.call-done) | copy-start | bytes 1572868
  151.4 106.3 %all-reduce.13.cloned.1.call-start = ((), (), s32[]{:S(2)}) async-start(), calls=%async_computation.6 | async-start | bytes 1048576 | tf_op jit(solution)/shard_map/psum | solution.py:62
  215.3 44.0 %copy-start.7 = (s32[1024]{0:T(1024)S(1)}, s32[1024]{0:T(1024)}, u32[]{:S(2)}) copy-start(s32[1024]{0:T(1024)} %param.8) | copy-start | bytes 12292
  219.1 98.6 %all-to-all-start.2 = ((f32[8,128,128]{2,1,0:T(8,128)}), f32[8,128,128]{2,1,0:T(8,128)}, u32[]{:S(2)}, u32[]{:S(2)}) async-start(f32[8,128,128]{2,1,0:T(8,128)} %bitcast.14), calls=%async_computation.2 | async-start | bytes 1048576 | tf_op jit(solution)/shard_map/all_to_all | solution.py:55
  223.3 94.4 %all-reduce.15.cloned.1.call-start = ((), (), s32[]{:S(2)}) async-start(), calls=%async_computation.7 | async-start | bytes 1048576 | tf_op jit(solution)/shard_map/psum | solution.py:53
  261.4 104.3 %all-reduce.17.cloned.1.call-start = ((), (), s32[]{:S(2)}) async-start(), calls=%async_computation.8 | async-start | bytes 1048576 | tf_op jit(solution)/shard_map/psum | solution.py:62
  320.9 46.7 %copy-start = (f32[2,128,128]{2,1,0:T(8,128)}, f32[2,128,128]{2,1,0:T(8,128)S(1)}, u32[]{:S(2)}) copy-start(f32[2,128,128]{2,1,0:T(8,128)S(1)} %bitcast_dynamic-update-slice_fusion) | copy-start | bytes 393220
Sparse Core Ops, SparseCore 0:
  38.1 57.5 all-reduce.6
  100.5 44.3 all-reduce.8
  151.5 56.1 all-reduce.10
  213.3 44.2 all-reduce.12
  261.5 56.1 all-reduce.14
  321.4 44.3 all-reduce.16
